TPU v7x, 768 devices: a whole 4x8x12 slice. The times are simulated.
768 devices in a mesh: seq: 192 (over z, y_lo, x, core), dp: 4 (over y_hi).
Axes of the slice: x: 4, y: 8 (y_hi: 4, y_lo: 2; y = y_hi * 2 + y_lo), z: 12, core: 2. Of those that a mesh axis runs over, the one named last changes fastest.
Arguments:
- queries: bfloat16 [4, 24576, 4096], P('dp', 'seq'), may hold values from -4.5 to 4.5
- context: bfloat16 [4, 24576, 1024], P('dp', 'seq'), may hold values from -4.5 to 4.5
- segment_start: int32 [4, 24576], P('dp', 'seq'), may hold values from 0 to 24575, as said below
- memory: bfloat16 [4, 192, 64, 1024], P('dp', 'seq'), may hold values from -4.5 to 4.5
- image_offset: int32 [4, 192], P('dp', 'seq'), may hold values from 0 to 128, as said below
- cross_gate: float32 [32], replicated, may hold values from -1.5 to 1.5
- out_grad: bfloat16 [4, 24576, 4096], P('dp', 'seq'), may hold values from -6 to 6
Outputs:
- query_grad: bfloat16 [4, 24576, 4096], P('dp', 'seq')
- context_grad: bfloat16 [4, 24576, 1024], P('dp', 'seq')
- memory_grad: bfloat16 [4, 192, 64, 1024], P('dp', 'seq')
- gate_grad: float32 [32], replicated
Inputs may be any that keep to these rules, and one draw needn't show every extreme that they name: `segment_start`: position of the first token of each token's segment: non-decreasing, equal to the position itself at a segment's first token; positions 0 and 24575 begin segments. `image_offset`: in each aligned block of 4 shards exactly one shard owns an image (offset below 128); every token that reads an image reads one owned at most 7 shards before its own, and that distance is reached in every draw.
All inputs are finite; a program needn't handle non-finite values.
Results may differ from a plain program's by a relative error of at most 0.012.
The roundings to bfloat16 on the way count: a program that leaves them out, or rounds other values in their place, can miss the bound.
Values may be sent and summed in bfloat16 or wider, within the bound.
A program may use at most 128 MiB of HBM per device.

v0:
```python
import math

import jax
import jax.numpy as jnp
from jax import lax
from jax.sharding import PartitionSpec as P

HEAD_DIM = 128
WINDOW = 64


def from_behind(shard, axis, by):
    size = lax.axis_size(axis)
    pairs = [(i, i + by) for i in range(size) if 0 <= i + by < size]
    return lax.ppermute(shard, axis, pairs)


def prefix(shard, axis, combine, identity, reverse):
    size, place = (lax.axis_size(axis), lax.axis_index(axis))
    everything = jax.tree.map(lambda part: lax.all_gather(part, axis), shard)
    start = jax.tree.map(
        lambda part, zero: jnp.broadcast_to(jnp.asarray(zero, part.dtype), part.shape),
        shard,
        identity,
    )

    def step(k, before):
        at = size - 1 - k if reverse else k
        reached = at > place if reverse else at < place
        new = combine(before, jax.tree.map(lambda part: part[at], everything))
        return jax.tree.map(lambda a, b: jnp.where(reached, a, b), new, before)

    return lax.fori_loop(0, size, step, start)


def masked_softmax(scores, allowed):
    scores = jnp.where(allowed, scores, -1e30)
    row_top = jnp.max(scores, axis=-1, keepdims=True)
    powers = jnp.exp(scores - row_top)
    return powers / jnp.sum(powers, axis=-1, keepdims=True)


def attend(query_rows, key_part, value_part, allowed):
    score_scale = 1.0 / math.sqrt(HEAD_DIM)
    scores = (
        jnp.einsum("gqd,gkd->gqk", query_rows, key_part, preferred_element_type=jnp.float32)
        * score_scale
    )
    weights = masked_softmax(scores, allowed[None])
    narrow_weights = weights.astype(jnp.bfloat16)
    mixed = jnp.einsum(
        "gqk,gkd->gqd", narrow_weights, value_part, preferred_element_type=jnp.float32
    )
    return (weights, narrow_weights, mixed)


def attend_back(grad_mixed, query_rows, key_part, value_part, weights, narrow_weights):
    score_scale = 1.0 / math.sqrt(HEAD_DIM)
    grad_weights = jnp.einsum(
        "gqd,gkd->gqk", grad_mixed, value_part, preferred_element_type=jnp.float32
    )
    row_delta = jnp.sum(weights * grad_weights, axis=-1, keepdims=True)
    grad_scores = (weights * (grad_weights - row_delta)).astype(jnp.bfloat16)
    grad_queries = (
        jnp.einsum("gqk,gkd->gqd", grad_scores, key_part, preferred_element_type=jnp.float32)
        * score_scale
    )
    grad_keys = (
        jnp.einsum("gqk,gqd->gkd", grad_scores, query_rows, preferred_element_type=jnp.float32)
        * score_scale
    )
    grad_values = jnp.einsum(
        "gqk,gqd->gkd", narrow_weights, grad_mixed, preferred_element_type=jnp.float32
    )
    return (grad_queries, grad_keys, grad_values)


def split_pair(joined, groups):
    key_width = groups * HEAD_DIM
    key_part = joined[:, :key_width].reshape(-1, groups, HEAD_DIM).transpose(1, 0, 2)
    value_part = joined[:, key_width:].reshape(-1, groups, HEAD_DIM).transpose(1, 0, 2)
    return (key_part, value_part)


def to_rows(values, groups, repeat):
    tok_rows = values.shape[0]
    return (
        values.reshape(tok_rows, groups, repeat, HEAD_DIM)
        .transpose(1, 2, 0, 3)
        .reshape(groups, repeat * tok_rows, HEAD_DIM)
    )


def from_rows(values, tok_rows):
    groups = values.shape[0]
    repeat = values.shape[1] // tok_rows
    return (
        values.reshape(groups, repeat, tok_rows, HEAD_DIM)
        .transpose(2, 0, 1, 3)
        .reshape(tok_rows, -1)
    )


def joined_terms(key_grad, value_grad):
    key_rows = key_grad.shape[1]
    return jnp.concatenate(
        [
            key_grad.transpose(1, 0, 2).reshape(key_rows, -1),
            value_grad.transpose(1, 0, 2).reshape(key_rows, -1),
        ],
        axis=1,
    )


def pick_later(earlier_part, later_part):
    chosen = jnp.where(later_part[1][0] > 0, later_part[0], earlier_part[0])
    return (chosen, jnp.maximum(earlier_part[1], later_part[1]))


def add_run(earlier_part, later_part):
    summed = later_part[0] + (1.0 - later_part[1][0]) * earlier_part[0]
    return (summed, jnp.maximum(earlier_part[1], later_part[1]))


def on_device(queries, context, segment_start, memory, image_offset, cross_gate, out_grad):
    tok_rows = queries.shape[1]
    key_width = context.shape[2] // 2
    groups = key_width // HEAD_DIM
    repeat = cross_gate.shape[0] // groups
    image_rows = memory.shape[2]
    shard_index = lax.axis_index("seq")
    query_rows = to_rows(queries[0], groups, repeat)
    earlier = from_behind(context[0][tok_rows - WINDOW :], "seq", 1)
    joined_keys = jnp.concatenate([earlier, context[0]], axis=0)
    key_part, value_part = split_pair(joined_keys, groups)
    query_pos = shard_index * tok_rows + jnp.arange(tok_rows, dtype=jnp.int32)
    key_pos = shard_index * tok_rows - WINDOW + jnp.arange(WINDOW + tok_rows, dtype=jnp.int32)
    segment_row = segment_start[0]
    allowed = (
        (key_pos[None, :] <= query_pos[:, None])
        & (key_pos[None, :] >= query_pos[:, None] - WINDOW)
        & (key_pos[None, :] >= segment_row[:, None])
    )
    allowed = jnp.tile(allowed, (repeat, 1))
    own_image = memory[0, 0]
    own_offset = image_offset[0, 0]
    is_owner = own_offset < tok_rows
    own_flag = is_owner.astype(jnp.bfloat16).reshape(1)
    before, before_flag = prefix(
        (own_image, own_flag),
        "seq",
        pick_later,
        (jnp.zeros_like(own_image), jnp.zeros_like(own_flag)),
        False,
    )
    has_prev = before_flag[0] > 0
    local = jnp.arange(tok_rows, dtype=jnp.int32)
    use_own = is_owner & (local >= own_offset)
    use_prev = jnp.logical_not(use_own) & has_prev
    columns = jnp.arange(2 * image_rows, dtype=jnp.int32)
    cross_allowed = jnp.where(columns[None, :] < image_rows, use_prev[:, None], use_own[:, None])
    cross_allowed = jnp.tile(cross_allowed, (repeat, 1))
    has_image = (use_own | use_prev).astype(jnp.float32)
    image_mask = jnp.tile(has_image, repeat)[None, :, None]
    weights, narrow_weights, mixed = attend(query_rows, key_part, value_part, allowed)
    self_out = mixed.astype(jnp.bfloat16)
    joined_memory = jnp.concatenate([before, own_image], axis=0)
    memory_keys, memory_values = split_pair(joined_memory, groups)
    cross_weights, cross_narrow, cross_mixed = attend(
        self_out, memory_keys, memory_values, cross_allowed
    )
    cross_mixed = cross_mixed * image_mask
    gate_tanh = jnp.tanh(cross_gate)
    grad_out = to_rows(out_grad[0], groups, repeat).astype(jnp.float32)
    gate_part = jnp.sum(
        (grad_out * cross_mixed).reshape(groups, repeat, tok_rows, HEAD_DIM), axis=(2, 3)
    ).reshape(-1)
    gate_rows = jnp.repeat(gate_tanh.reshape(groups, repeat), tok_rows, axis=1)[:, :, None]
    grad_cross = (grad_out * gate_rows * image_mask).astype(jnp.bfloat16)
    cross_query_grad, memory_key_grad, memory_value_grad = attend_back(
        grad_cross, self_out, memory_keys, memory_values, cross_weights, cross_narrow
    )
    grad_self = (grad_out + cross_query_grad).astype(jnp.bfloat16)
    query_grad, key_grad, value_grad = attend_back(
        grad_self, query_rows, key_part, value_part, weights, narrow_weights
    )
    key_terms = joined_terms(key_grad, value_grad)
    returned = from_behind(key_terms[:WINDOW], "seq", -1)
    context_grad = (
        key_terms[WINDOW:] + jnp.pad(returned, ((tok_rows - WINDOW, 0), (0, 0)))
    ).astype(jnp.bfloat16)[None]
    image_terms = joined_terms(memory_key_grad, memory_value_grad)
    carried = image_terms[:image_rows]
    owner_weight = is_owner.astype(jnp.float32).reshape(1)
    arrived, flag_total = prefix(
        (carried, owner_weight),
        "seq",
        add_run,
        (jnp.zeros_like(carried), jnp.zeros_like(owner_weight)),
        True,
    )
    memory_grad = jnp.where(is_owner, image_terms[image_rows:] + arrived, 0.0).astype(jnp.bfloat16)[
        None, None
    ]
    gate_total = lax.psum(gate_part, ("seq", "dp"))
    gate_grad = (1.0 - gate_tanh * gate_tanh) * gate_total
    return (
        from_rows(query_grad, tok_rows).reshape(1, tok_rows, -1).astype(jnp.bfloat16),
        context_grad,
        memory_grad,
        gate_grad,
    )


def solution(mesh):
    placed = (
        P("dp", "seq", None),
        P("dp", "seq", None),
        P("dp", "seq"),
        P("dp", "seq", None, None),
        P("dp", "seq"),
        P(),
        P("dp", "seq", None),
    )
    return jax.shard_map(
        on_device,
        mesh=mesh,
        in_specs=placed,
        out_specs=(P("dp", "seq", None), P("dp", "seq", None), P("dp", "seq", None, None), P()),
        check_vma=False,
    )
```

profile of v0, /device:TPU:1, one launch (start us, length us, event | category | flops | bytes accessed | tf_op | source)
XLA Modules:
  0.0 2047.1 jit_solution(3716083404511855888)
XLA Ops:
  9.5 4.5 collective-permute-start
  18.7 2.0 copy.79
  25.2 422.6 %all-reduce.1 = bf16[192]{0:T(256)(128)(2,1)S(1)} all-reduce(bf16[192]{0:T(256)(128)(2,1)S(1)} %dynamic-update-slice), channel_id=1, replica_groups=mesh['seq'=192,'dp'=4] {'seq'}, use_global_device_ids=true, to_apply=%add.1 | all-reduce | flops 192 | bytes 768
  448.4 1.8 fusion.27
  450.2 3.9 fusion.56
  454.1 3.8 convolution_convert_fusion
  457.9 556.7 %while.32 = (s32[]{:T(128)}, bf16[64,1024]{1,0:T(8,128)(2,1)S(1)}, bf16[1]{0:T(256)(128)(2,1)}, s32[]{:T(128)}, bf16[192,1]{0,1:T(2,128)(2,1)S(1)}, /*index=5*/bf16[192,64,1024]{2,1,0:T(8,128)(2,1)}, s32[]{:T(128)}, s32[]{:T(128)}) while((s32[]{:T(128)}, bf16[64,1024]{1,0:T(8,128)(2,1)S(1)}, bf16[1]{0:T(256)(128)(2,1)}, s32[]{:T(128)}, ...), condition=%wide.region_3.4_spmd.clone, body=%wide.region_2.3_spmd.clone.sunk | while | flops 196617 | bytes 393356 | solution.py:33
  1015.3 3.5 fusion.57
  1018.8 2.1 multiply_reduce_fusion.1
  1021.1 109.6 %psum.7 = f32[32]{0:T(128)S(1)} all-reduce(f32[32]{0:T(128)S(1)} %reshape.255), channel_id=1, replica_groups=mesh['seq'=192,'dp'=4] {'seq','dp'}, use_global_device_ids=true, to_apply=%region_12.13 | all-reduce | flops 32 | bytes 256 | tf_op jit(solution)/shard_map/psum | solution.py:205
  1131.4 2.2 fusion.16
  1133.7 2.5 multiply_reduce_fusion.2
  1136.3 2.8 multiply_convert_fusion.2
  1144.4 2.0 dynamic-update-slice.1
  1146.3 417.0 %all-reduce.2 = f32[192]{0:T(256)} all-reduce(f32[192]{0:T(256)} %dynamic-update-slice.1), channel_id=1, replica_groups=mesh['seq'=192,'dp'=4] {'seq'}, use_global_device_ids=true, to_apply=%add.2 | all-reduce | flops 192 | bytes 1536
  1568.4 2.3 collective-permute-start.1
  1573.9 2.3 collective-permute-done.1
  1577.9 461.7 %while.33 = (s32[]{:T(128)}, f32[64,1024]{1,0:T(8,128)S(1)}, s32[]{:T(128)}, f32[192,64,1024]{2,1,0:T(8,128)}, f32[192,1]{0,1:T(1,128)S(1)}, /*index=5*/s32[]{:T(128)}, s32[]{:T(128)}, s32[]{:T(128)}, s32[]{:T(128)}) while((s32[]{:T(128)}, f32[64,1024]{1,0:T(8,128)S(1)}, s32[]{:T(128)}, f32[192,64,1024]{2,1,0:T(8,128)}, ...), condition=%wide.region_9.10_spmd.clone, body=%wide.region_8.9_spmd.clone.sunk | while | flops 262153 | bytes 786619 | solution.py:33
  1578.5 1.8 fusion.77
  1580.9 1.8 fusion.77
  1595.3 1.8 fusion.77
  1609.7 1.8 fusion.77
  1624.2 1.8 fusion.77
  1626.6 1.8 fusion.77
  1641.0 1.8 fusion.77
  1655.4 1.8 fusion.77
  1669.9 1.8 fusion.77
  1672.3 1.8 fusion.77
  1686.7 1.8 fusion.77
  1701.1 1.8 fusion.77
  1715.5 1.8 fusion.77
  1717.9 1.8 fusion.77
  (846 shorter events, 885.4 us)
Async XLA Ops:
  7.2 9.5 copy-start.14
  7.2 450.7 %all-gather.5.cloned.1.call-start = ((), (), s32[]{:S(2)}) async-start(), calls=%async_computation | async-start | bytes 25296896 | tf_op jit(solution)/shard_map/all_gather | solution.py:20
  7.9 1569.9 %all-gather.7.cloned.1.call-start = ((), (), s32[]{:S(2)}) async-start(), calls=%async_computation.1 | async-start | bytes 50593792 | tf_op jit(solution)/shard_map/all_gather | solution.py:20
  9.5 438.8 %collective-permute-start = (bf16[64,1024]{1,0:T(8,128)(2,1)}, bf16[64,1024]{1,0:T(8,128)(2,1)}, u32[]{:S(2)}, u32[]{:S(2)}) collective-permute-start(bf16[64,1024]{1,0:T(8,128)(2,1)} %slice_bitcast_fusion), channel_id=1, source_target_pairs={{0,4},{4,8},{8,12},{12,16},{16,20},{20,24},{24,28},{28,32},{32,36}... | collective-permute-start | bytes 393224 | tf_op jit(solution)/shard_map/ppermute | solution.py:15
  14.1 3.6 copy-start.7
  18.3 431.8 %copy-start = (bf16[4,8,128,128]{3,2,1,0:T(8,128)(2,1)}, bf16[4,8,128,128]{3,2,1,0:T(8,128)(2,1)S(1)}, u32[]{:S(2)}) copy-start(bf16[4,8,128,128]{3,2,1,0:T(8,128)(2,1)S(1)} %copy.78) | copy-start | bytes 3145732
  454.1 3.8 copy-start.12
  1018.8 114.9 %copy-start.11 = (f32[4,1024]{1,0:T(4,128)}, f32[4,1024]{1,0:T(4,128)S(1)}, u32[]{:S(2)}) copy-start(f32[4,1024]{1,0:T(4,128)S(1)} %get-tuple-element.322) | copy-start | bytes 49156
  1018.8 111.8 %copy-start.15 = (f32[32]{0:T(128)S(1)}, f32[32]{0:T(128)}, u32[]{:S(2)}) copy-start(f32[32]{0:T(128)} %param.16) | copy-start | bytes 388
  1131.4 2.2 copy-start.6
  1136.3 5.9 copy-start.3
  1136.3 2.9 copy-start.8
  1563.4 1.9 copy-start.2
  1563.4 1.9 copy-start.10
  1565.8 1.2 copy-start.1
  1567.7 2.9 copy-start.9
  1568.4 7.8 collective-permute-start.1
  1572.6 5.2 copy-start.13
  1577.9 461.7 %copy-start.4 = (f32[128,512]{1,0:T(8,128)S(1)}, f32[128,512]{1,0:T(8,128)}, u32[]{:S(2)}) copy-start(f32[128,512]{1,0:T(8,128)} %copy-done.3) | copy-start | bytes 786436
  1577.9 461.7 %copy-start.5 = (f32[128,512]{1,0:T(8,128)S(1)}, f32[128,512]{1,0:T(8,128)}, u32[]{:S(2)}) copy-start(f32[128,512]{1,0:T(8,128)} %copy.97) | copy-start | bytes 786436
Sparse Core Ops, SparseCore 0:
  10.5 351.9 all-gather.4
  1143.9 374.3 all-gather.6
where the time goes:
time: 2060 us; the launch traced here: 2050 us
  blocking collectives  949 us (46%)
  other arithmetic  894 us (43%)
  loops' own time  137 us (7%)
  matrix products  21.8 us (1%)
  local copies, waits for them, and re-layouts  20.9 us (1%)
    unnamed x2, blocking collectives  840 us
    select_n x384, other arithmetic, step(): return jax.tree.map(lambda a, b: jnp.where(reached, a, b), new, before)  655 us
    another operation x2, loops' own time, prefix(): return lax.fori_loop(0, size, step, start)  137 us
    gt x192, other arithmetic, pick_later(): chosen = jnp.where(later_part[1][0] > 0, later_part[0], earlier_part[0])  114 us
    sub x192, other arithmetic, add_run(): summed = later_part[0] + (1.0 - later_part[1][0]) * earlier_part[0]  113 us
    psum x1, blocking collectives, on_device(): gate_total = lax.psum(gate_part, ('seq', 'dp'))  110 us
  transfers between devices with their start and end apart: 4, of which 1 were waited for; matrix products, arithmetic and copies ran while one was open for 2% of the time, Pallas kernels for 0%

commit v1 on v0

v1 whole, which is shorter than its diff:
```python
import functools
import math

import jax
import jax.numpy as jnp
from jax import lax
from jax.experimental import pallas as pl
from jax.experimental.pallas import tpu as pltpu
from jax.sharding import PartitionSpec as P

HEAD_DIM = 128
WINDOW = 64
BLOCK = 4
ROW = 8
SCALE = 1.0 / math.sqrt(HEAD_DIM)
EXP_SCALE = SCALE / math.log(2.0)
MESH = pl.DeviceIdType.MESH
F32 = jnp.float32
BF16 = jnp.bfloat16
HIDDEN = -1e30


def dot_nn(a, b):
    return lax.dot_general(a, b, (((1,), (0,)), ((), ())), preferred_element_type=F32)


def dot_nt(a, b):
    return lax.dot_general(a, b, (((1,), (1,)), ((), ())), preferred_element_type=F32)


def dot_tn(a, b):
    return lax.dot_general(a, b, (((0,), (0,)), ((), ())), preferred_element_type=F32)


def softmax(scores):
    top = jnp.max(scores, axis=-1, keepdims=True)
    powers = jnp.exp2((scores - top) * EXP_SCALE)
    return powers * (1.0 / jnp.sum(powers, axis=-1, keepdims=True))


def stacked(ref, half, group, repeat):
    base = group * (repeat * HEAD_DIM)
    rows = slice(half * WINDOW, (half + 1) * WINDOW)
    return jnp.concatenate(
        [
            ref[rows, pl.ds(pl.multiple_of(base + head * HEAD_DIM, HEAD_DIM), HEAD_DIM)]
            for head in range(repeat)
        ],
        axis=0,
    )


def columns(group, offset=0):
    return pl.ds(pl.multiple_of(offset + group * HEAD_DIM, HEAD_DIM), HEAD_DIM)


def kernel(
    shards,
    docs,
    seg_ref,
    off_ref,
    gate_ref,
    q_hbm,
    c_hbm,
    m_hbm,
    g_hbm,
    qg_hbm,
    cg_hbm,
    mg_hbm,
    gt_ref,
    q_buf,
    g_buf,
    keys,
    images,
    cur_buf,
    prev_buf,
    scat_buf,
    flag_own,
    flag_buf,
    w_ref,
    so_ref,
    gs_ref,
    bias_ref,
    cbias_ref,
    has_ref,
    tanh_ref,
    gacc_ref,
    mt_ref,
    kt_ref,
    qg_buf,
    cg_buf,
    mg_buf,
    to_cur,
    to_prev,
    red_cur,
    red_prev,
    sum_buf,
    halo_out,
    halo_in,
    ga_own,
    ga_in,
    gb_own,
    gb_in,
    gc_own,
    gc_in,
    local_sem,
    send_sem,
    recv_sem,
):
    heads = gate_ref.shape[1]
    tok_rows = q_buf.shape[0]
    width = keys.shape[1]
    key_width = width // 2
    groups = key_width // HEAD_DIM
    repeat = heads // groups
    quarter = m_hbm.shape[0] // BLOCK
    image_rows = m_hbm.shape[0]
    tall = repeat * WINDOW

    me = lax.axis_index("seq")
    doc = lax.axis_index("dp")
    place = lax.rem(me, BLOCK)
    block = me // BLOCK
    blocks = shards // BLOCK
    next_block = lax.rem(block + 1, blocks)
    last_block = lax.rem(block + blocks - 1, blocks)
    y_count = 2 * docs
    z_count = shards // (2 * ROW)
    in_row = lax.rem(me, ROW)
    y_place = doc * 2 + lax.rem(me // ROW, 2)
    z_place = me // (2 * ROW)

    def mate(d):
        return lax.rem(place + d, BLOCK)

    def on_seq(index):
        return {"seq": index, "dp": doc}

    def in_block(which, d):
        return on_seq(which * BLOCK + mate(d))

    def row_peer(d):
        return on_seq(me - in_row + lax.rem(in_row + d, ROW))

    def y_peer(d):
        there = lax.rem(y_place + d, y_count)
        return {
            "seq": z_place * (2 * ROW) + lax.rem(there, 2) * ROW + in_row,
            "dp": there // 2,
        }

    def z_peer(d):
        there = lax.rem(z_place + d, z_count)
        return on_seq(there * (2 * ROW) + lax.rem(me, 2 * ROW))

    sems = [0]

    def remote(src, dst, device):
        at = sems[0]
        sems[0] += 1
        return pltpu.make_async_remote_copy(
            src_ref=src,
            dst_ref=dst,
            send_sem=send_sem.at[at],
            recv_sem=recv_sem.at[at],
            device_id=device,
            device_id_type=MESH,
        )

    barrier = pltpu.get_barrier_semaphore()
    greeted = (
        [in_block(block, d) for d in range(1, BLOCK)]
        + [in_block(next_block, d) for d in range(BLOCK)]
        + [in_block(last_block, d) for d in range(BLOCK)]
        + [y_peer(d) for d in range(1, y_count)]
        + [z_peer(d) for d in range(1, z_count)]
    )
    for device in greeted:
        pl.semaphore_signal(barrier, inc=1, device_id=device, device_id_type=MESH)

    load_keys = pltpu.make_async_copy(
        c_hbm, keys.at[pl.ds(WINDOW, tok_rows)], local_sem.at[0]
    )
    load_q = pltpu.make_async_copy(q_hbm, q_buf, local_sem.at[1])
    load_own = pltpu.make_async_copy(
        m_hbm, images.at[pl.ds(image_rows, image_rows)], local_sem.at[2]
    )
    load_g = pltpu.make_async_copy(g_hbm, g_buf, local_sem.at[3])
    load_keys.start()
    load_q.start()
    load_own.start()
    load_g.start()

    offset = off_ref[0, 0]
    flag_own[...] = jnp.where(jnp.full(flag_own.shape, offset, jnp.int32) < tok_rows, 1.0, 0.0)
    pl.semaphore_wait(barrier, len(greeted))

    flags = [remote(flag_own, flag_buf.at[d - 1], in_block(block, d)) for d in range(1, BLOCK)]
    scatter = [
        remote(
            m_hbm.at[pl.ds(pl.multiple_of(mate(d) * quarter, quarter), quarter)],
            scat_buf.at[d - 1],
            in_block(block, d),
        )
        for d in range(1, BLOCK)
    ]
    halo = remote(
        c_hbm.at[pl.ds(tok_rows - WINDOW, WINDOW)],
        keys.at[pl.ds(0, WINDOW)],
        on_seq(lax.rem(me + 1, shards)),
    )
    for copy in flags + scatter + [halo]:
        copy.start()

    row_id = lax.broadcasted_iota(jnp.int32, (WINDOW, 2 * WINDOW), 0)
    col_id = lax.broadcasted_iota(jnp.int32, (WINDOW, 2 * WINDOW), 1)
    band = (col_id >= row_id) & (col_id <= row_id + WINDOW)
    wide_row = lax.broadcasted_iota(jnp.int32, (tok_rows, tok_rows), 0)
    wide_col = lax.broadcasted_iota(jnp.int32, (tok_rows, tok_rows), 1)
    starts = jnp.sum(
        jnp.where(
            wide_row == wide_col,
            jnp.broadcast_to(seg_ref[...].astype(F32), (tok_rows, tok_rows)),
            0.0,
        ),
        axis=1,
        keepdims=True,
    )
    starts = starts - (me * tok_rows).astype(F32)
    for half in range(2):
        begin = starts[half * WINDOW : (half + 1) * WINDOW]
        key_at = (col_id - (WINDOW if half == 0 else 0)).astype(F32)
        bias_ref[half] = jnp.where(band & (key_at >= begin), 0.0, HIDDEN)
    gate_row = gate_ref[...]
    head_eye = lax.broadcasted_iota(jnp.int32, (heads, heads), 0) == lax.broadcasted_iota(
        jnp.int32, (heads, heads), 1
    )
    gate_col = jnp.sum(
        jnp.where(head_eye, jnp.broadcast_to(gate_row, (heads, heads)), 0.0), axis=1, keepdims=True
    )
    tanh_ref[...] = jnp.tanh(jnp.broadcast_to(gate_col, tanh_ref.shape))

    def self_forward(half, group):
        query = stacked(q_buf, half, group, repeat)
        first = half * WINDOW
        key = keys[first : first + 2 * WINDOW, columns(group)]
        value = keys[first : first + 2 * WINDOW, columns(group, key_width)]
        scores = dot_nt(query, key).reshape(repeat, WINDOW, 2 * WINDOW) + bias_ref[half][None]
        weights = softmax(scores.reshape(tall, 2 * WINDOW))
        w_ref[half, group] = weights
        so_ref[half, group] = dot_nn(weights.astype(BF16), value).astype(BF16)

    load_keys.wait()
    load_q.wait()

    @pl.loop(0, groups)
    def _(group):
        self_forward(1, group)

    for copy in flags + scatter:
        copy.wait_recv()
    load_own.wait()
    own_flag = flag_own[0:1, 0:1]
    picked = own_flag * images[
        pl.ds(pl.multiple_of(image_rows + place * quarter, quarter), quarter), :
    ].astype(F32)
    earlier = jnp.zeros((1, 1), F32)
    for d in range(1, BLOCK):
        flag = flag_buf[d - 1, 0:1, 0:1]
        picked = picked + flag * scat_buf[d - 1].astype(F32)
        earlier = earlier + flag * jnp.where(place >= d, 1.0, 0.0)
    mine = pl.ds(pl.multiple_of(place * quarter, quarter), quarter)
    cur_buf[mine, :] = picked.astype(BF16)
    gather = [
        remote(cur_buf.at[mine], cur_buf.at[mine], in_block(block, d)) for d in range(1, BLOCK)
    ]
    onward = [
        remote(cur_buf.at[mine], prev_buf.at[mine], in_block(next_block, d)) for d in range(BLOCK)
    ]
    for copy in onward + gather:
        copy.start()

    halo.wait_recv()

    @pl.loop(0, groups)
    def _(group):
        self_forward(0, group)

    is_owner = own_flag > 0.5
    has_prev = jnp.maximum(earlier, jnp.where(block > 0, 1.0, 0.0))
    local_row = row_id.astype(F32)
    image_col = col_id < image_rows
    for half in range(2):
        at = local_row + float(half * WINDOW)
        use_own = jnp.where(at >= offset.astype(F32), own_flag, 0.0)
        use_prev = (1.0 - use_own) * has_prev
        cbias_ref[half] = (jnp.where(image_col, use_prev, use_own) - 1.0) * (-HIDDEN)
        has_ref[half] = jnp.maximum(use_own, use_prev)

    for copy in gather + onward:
        copy.wait_recv()
    load_g.wait()
    images[0:image_rows, :] = (
        earlier * cur_buf[...].astype(F32) + (1.0 - earlier) * prev_buf[...].astype(F32)
    ).astype(BF16)

    def cross_half(half, group, key, value):
        self_out = so_ref[half, group]
        grad_out = stacked(g_buf, half, group, repeat)
        scores = dot_nt(self_out, key).reshape(repeat, WINDOW, 2 * image_rows) + cbias_ref[half][None]
        weights = softmax(scores.reshape(tall, 2 * image_rows)).reshape(
            repeat, WINDOW, 2 * image_rows
        )
        narrow = weights.astype(BF16)
        raw = dot_nt(grad_out, value).reshape(repeat, WINDOW, 2 * image_rows)
        has = has_ref[half][None]
        gate_sum = jnp.sum(narrow.astype(F32) * raw * has, axis=1)
        factor = has * tanh_ref[pl.ds(pl.multiple_of(group * repeat, repeat), repeat), :][:, None, :]
        grad_wide = grad_out.astype(F32)
        grad_cross = (grad_wide.reshape(factor.shape) * factor).astype(BF16).reshape(tall, HEAD_DIM)
        grad_weights = raw * factor
        delta = jnp.sum(weights * grad_weights, axis=-1, keepdims=True)
        grad_scores = (
            (weights * (grad_weights - delta)).astype(BF16).reshape(tall, 2 * image_rows)
        )
        query_grad = dot_nn(grad_scores, key) * SCALE
        gs_ref[half, group] = (grad_wide + query_grad).astype(BF16)
        key_term = dot_tn(grad_scores, self_out)
        value_term = dot_tn(narrow.reshape(tall, 2 * image_rows), grad_cross)
        return gate_sum, key_term, value_term

    @pl.loop(0, groups)
    def _(group):
        key = images[:, columns(group)]
        value = images[:, columns(group, key_width)]
        first = cross_half(0, group, key, value)
        second = cross_half(1, group, key, value)
        gacc_ref[pl.ds(pl.multiple_of(group * repeat, repeat), repeat), :] = first[0] + second[0]
        mt_ref[:, columns(group)] = (first[1] + second[1]) * SCALE
        mt_ref[:, columns(group, key_width)] = first[2] + second[2]

    totals = jnp.sum(gacc_ref[...], axis=1, keepdims=True)
    spread = lax.broadcasted_iota(jnp.int32, (heads, 128), 0) == lax.broadcasted_iota(
        jnp.int32, (heads, 128), 1
    )
    gate_line = jnp.sum(jnp.where(spread, totals, 0.0), axis=0, keepdims=True)
    ga_own[...] = jnp.broadcast_to(gate_line, ga_own.shape)
    ga = [remote(ga_own, ga_in.at[d - 1], row_peer(d)) for d in range(1, ROW)]
    for copy in ga:
        copy.start()

    carried = mt_ref[0:image_rows, :]
    to_cur[...] = (carried * earlier).astype(BF16)
    to_prev[...] = (carried * (1.0 - earlier)).astype(BF16)

    def part(d):
        return pl.ds(pl.multiple_of(mate(d) * quarter, quarter), quarter)

    reduce_prev = [
        remote(to_prev.at[part(d)], red_prev.at[d], in_block(last_block, d)) for d in range(BLOCK)
    ]
    reduce_cur = [
        remote(to_cur.at[part(d)], red_cur.at[d - 1], in_block(block, d)) for d in range(1, BLOCK)
    ]
    for copy in reduce_prev + reduce_cur:
        copy.start()

    def self_backward(half, group):
        query = stacked(q_buf, half, group, repeat)
        first = half * WINDOW
        key = keys[first : first + 2 * WINDOW, columns(group)]
        value = keys[first : first + 2 * WINDOW, columns(group, key_width)]
        weights = w_ref[half, group]
        grad_self = gs_ref[half, group]
        grad_weights = dot_nt(grad_self, value)
        delta = jnp.sum(weights * grad_weights, axis=-1, keepdims=True)
        grad_scores = (weights * (grad_weights - delta)).astype(BF16)
        query_grad = (dot_nn(grad_scores, key) * SCALE).astype(BF16)
        base = group * (repeat * HEAD_DIM)
        for head in range(repeat):
            qg_buf[
                first : first + WINDOW,
                pl.ds(pl.multiple_of(base + head * HEAD_DIM, HEAD_DIM), HEAD_DIM),
            ] = query_grad[head * WINDOW : (head + 1) * WINDOW]
        kt_ref[half, :, columns(group)] = dot_tn(grad_scores, query) * SCALE
        kt_ref[half, :, columns(group, key_width)] = dot_tn(weights.astype(BF16), grad_self)

    @pl.loop(0, groups)
    def _(group):
        self_backward(0, group)

    halo_out[...] = kt_ref[0, 0:WINDOW, :].astype(BF16)
    halo_back = remote(halo_out, halo_in, on_seq(lax.rem(me + shards - 1, shards)))
    halo_back.start()
    out_low = pltpu.make_async_copy(
        qg_buf.at[pl.ds(0, WINDOW)], qg_hbm.at[pl.ds(0, WINDOW)], local_sem.at[4]
    )
    out_low.start()

    for copy in ga:
        copy.wait_recv()
    gate_line = ga_own[...]
    for d in range(1, ROW):
        gate_line = gate_line + ga_in[d - 1]
    gb_own[...] = gate_line
    gb = [remote(gb_own, gb_in.at[d - 1], y_peer(d)) for d in range(1, y_count)]
    for copy in gb:
        copy.start()

    for copy in reduce_cur + reduce_prev:
        copy.wait_recv()
    summed = to_cur[mine, :].astype(F32) + red_prev[0].astype(F32)
    for d in range(1, BLOCK):
        summed = summed + red_cur[d - 1].astype(F32) + red_prev[d].astype(F32)
    sum_buf[mine, :] = summed.astype(BF16)
    give = [
        remote(sum_buf.at[mine], sum_buf.at[mine], in_block(block, d)) for d in range(1, BLOCK)
    ]
    for copy in give:
        copy.start()

    @pl.loop(0, groups)
    def _(group):
        self_backward(1, group)

    out_high = pltpu.make_async_copy(
        qg_buf.at[pl.ds(WINDOW, WINDOW)], qg_hbm.at[pl.ds(WINDOW, WINDOW)], local_sem.at[5]
    )
    out_high.start()

    for copy in gb:
        copy.wait_recv()
    gate_line = gb_own[...]
    for d in range(1, y_count):
        gate_line = gate_line + gb_in[d - 1]
    gc_own[...] = gate_line
    gc = [remote(gc_own, gc_in.at[d - 1], z_peer(d)) for d in range(1, z_count)]
    for copy in gc:
        copy.start()

    halo_back.wait_recv()
    cg_buf[0:WINDOW, :] = (kt_ref[0, WINDOW : 2 * WINDOW, :] + kt_ref[1, 0:WINDOW, :]).astype(BF16)
    cg_buf[WINDOW : 2 * WINDOW, :] = (
        kt_ref[1, WINDOW : 2 * WINDOW, :] + halo_in[...].astype(F32)
    ).astype(BF16)
    out_context = pltpu.make_async_copy(cg_buf, cg_hbm, local_sem.at[6])
    out_context.start()

    for copy in give:
        copy.wait_recv()
    mg_buf[...] = (
        (mt_ref[image_rows : 2 * image_rows, :] + sum_buf[...].astype(F32)) * own_flag
    ).astype(BF16)
    out_memory = pltpu.make_async_copy(mg_buf, mg_hbm, local_sem.at[7])
    out_memory.start()

    for copy in gc:
        copy.wait_recv()
    gate_line = gc_own[...]
    for d in range(1, z_count):
        gate_line = gate_line + gc_in[d - 1]
    gate_tanh = jnp.tanh(gate_row)
    gt_ref[...] = (1.0 - gate_tanh * gate_tanh) * gate_line[0:1, 0:heads]

    for copy in (
        flags + scatter + [halo] + gather + onward + ga + reduce_prev + reduce_cur
        + [halo_back] + gb + give + gc
    ):
        copy.wait_send()
    out_low.wait()
    out_high.wait()
    out_context.wait()
    out_memory.wait()


def on_device(shards, docs, queries, context, segment_start, memory, image_offset, cross_gate, out_grad):
    tok_rows, model = queries.shape[1:]
    width = context.shape[2]
    image_rows = memory.shape[2]
    heads = cross_gate.shape[0]
    groups = width // 2 // HEAD_DIM
    repeat = heads // groups
    quarter = image_rows // BLOCK
    tall = repeat * WINDOW
    y_count = 2 * docs
    z_count = shards // (2 * ROW)
    copies = 3 + 3 + 1 + 3 + 4 + (ROW - 1) + 4 + 3 + 1 + (y_count - 1) + 3 + (z_count - 1)
    anywhere = pl.BlockSpec(memory_space=pl.ANY)
    vmem = pl.BlockSpec(memory_space=pltpu.VMEM)
    smem = pl.BlockSpec(memory_space=pltpu.SMEM)

    def buf(*shape):
        return pltpu.VMEM(shape, BF16)

    def wide(*shape):
        return pltpu.VMEM(shape, F32)

    query_grad, context_grad, memory_grad, gate_grad = pl.pallas_call(
        functools.partial(kernel, shards, docs),
        out_shape=(
            jax.ShapeDtypeStruct((tok_rows, model), BF16),
            jax.ShapeDtypeStruct((tok_rows, width), BF16),
            jax.ShapeDtypeStruct((image_rows, width), BF16),
            jax.ShapeDtypeStruct((1, heads), F32),
        ),
        in_specs=[vmem, smem, vmem, anywhere, anywhere, anywhere, anywhere],
        out_specs=(anywhere, anywhere, anywhere, vmem),
        scratch_shapes=[
            buf(tok_rows, model),
            buf(tok_rows, model),
            buf(WINDOW + tok_rows, width),
            buf(2 * image_rows, width),
            buf(image_rows, width),
            buf(image_rows, width),
            buf(BLOCK - 1, quarter, width),
            wide(8, 128),
            wide(BLOCK - 1, 8, 128),
            wide(2, groups, tall, 2 * WINDOW),
            buf(2, groups, tall, HEAD_DIM),
            buf(2, groups, tall, HEAD_DIM),
            wide(2, WINDOW, 2 * WINDOW),
            wide(2, WINDOW, 2 * image_rows),
            wide(2, WINDOW, 2 * image_rows),
            wide(heads, 128),
            wide(heads, 128),
            wide(2 * image_rows, width),
            wide(2, 2 * WINDOW, width),
            buf(tok_rows, model),
            buf(tok_rows, width),
            buf(image_rows, width),
            buf(image_rows, width),
            buf(image_rows, width),
            buf(BLOCK - 1, quarter, width),
            buf(BLOCK, quarter, width),
            buf(image_rows, width),
            buf(WINDOW, width),
            buf(WINDOW, width),
            wide(8, 128),
            wide(ROW - 1, 8, 128),
            wide(8, 128),
            wide(max(y_count - 1, 1), 8, 128),
            wide(8, 128),
            wide(max(z_count - 1, 1), 8, 128),
            pltpu.SemaphoreType.DMA((8,)),
            pltpu.SemaphoreType.DMA((copies,)),
            pltpu.SemaphoreType.DMA((copies,)),
        ],
        compiler_params=pltpu.CompilerParams(
            collective_id=0, has_side_effects=True, vmem_limit_bytes=60000 * 1024
        ),
    )(
        segment_start,
        image_offset,
        cross_gate.reshape(1, heads),
        queries[0],
        context[0],
        memory[0, 0],
        out_grad[0],
    )
    return query_grad[None], context_grad[None], memory_grad[None, None], gate_grad.reshape(heads)


def solution(mesh):
    placed = (
        P("dp", "seq", None),
        P("dp", "seq", None),
        P("dp", "seq"),
        P("dp", "seq", None, None),
        P("dp", "seq"),
        P(),
        P("dp", "seq", None),
    )
    return jax.shard_map(
        functools.partial(on_device, mesh.shape["seq"], mesh.shape["dp"]),
        mesh=mesh,
        in_specs=placed,
        out_specs=(P("dp", "seq", None), P("dp", "seq", None), P("dp", "seq", None, None), P()),
        check_vma=False,
    )
```

time: 2060 us -> 57.6 us (0.03)
  blocking collectives: 949 us -> 0 us
  other arithmetic: 894 us -> 0 us
  loops' own time: 137 us -> 0 us
  Pallas kernels: 0 us -> 51.6 us
  matrix products: 21.8 us -> 0 us
    unnamed x2 -> x0, blocking collectives: 840 us -> none
    select_n x385 -> x0, other arithmetic: 655 us -> none  [the longest x384 655 us: step(): return jax.tree.map(lambda a, b: jnp.where(reached, a, b), new, before)]
    another operation x2 -> x0, loops' own time: 137 us -> none  [prefix(): return lax.fori_loop(0, size, step, start)]
    gt x192 -> x0, other arithmetic: 114 us -> none  [pick_later(): chosen = jnp.where(later_part[1][0] > 0, later_part[0], earlier_part[0])]
    sub x192 -> x0, other arithmetic: 113 us -> none  [add_run(): summed = later_part[0] + (1.0 - later_part[1][0]) * earlier_part[0]]
    psum x1 -> x0, blocking collectives: 110 us -> none  [on_device(): gate_total = lax.psum(gate_part, ('seq', 'dp'))]
    pallas_call x0 -> x1, Pallas kernels: none -> 51.6 us  [on_device(): pl.pallas_call(functools.partial(kernel, shards, docs), out_shape=(jax.Sh...]
  transfers between devices with their start and end apart: 4 -> 0, of which waited for: 1 -> 0; matrix products, arithmetic and copies ran while one was open for 2% -> 0% of each run, Pallas kernels for 0% -> 0%
where the time goes in v1:
time: 57.6 us; the launch traced here: 57.4 us
  Pallas kernels  51.6 us (90%)
  local copies, waits for them, and re-layouts  4.51 us (8%)
  between operations  1.3 us (2%)
    pallas_call x1, Pallas kernels, on_device(): pl.pallas_call(functools.partial(kernel, shards, docs), out_shape=(jax.Sh...  51.6 us
    unnamed x10, local copies, waits for them, and re-layouts  4.51 us

profile of v1, /device:TPU:1, one launch (start us, length us, event | category | flops | bytes accessed | tf_op | source)
XLA Modules:
  0.0 57.4 jit_solution(14123718212768995739)
XLA Ops:
  1.3 51.6 %shard_map.102 = (bf16[128,4096]{1,0:T(8,128)(2,1)}, bf16[128,1024]{1,0:T(8,128)(2,1)}, bf16[64,1024]{1,0:T(8,128)(2,1)}, f32[1,32]{1,0:T(1,128)}) custom-call(s32[1,128]{1,0:T(1,128)} %seg_ref.1, s32[1,1]{1,0:T(1,128)S(6)} %copy.15.off_ref, f32[1,32]{1,0:T(1,128)} %bitcast.16, bf16[128,4096]{1,0:T(8,128)(2,1)} %bitcast.9, bf16[128,1024]{1,0:T(8,128)(2,1)} %bitcast.12, ...), custom_call_target="tpu_custom_call" | custom-call | tf_op jit(solution)/shard_map/pallas_call | solution.py:498
  52.9 0.0 copy-start
  52.9 2.3 %copy.16 = bf16[1,128,4096]{2,1,0:T(8,128)(2,1)} copy(bf16[1,128,4096]{2,1,0:T(8,128)(2,1)} %bitcast.11) | data formatting | bytes 2097152
  55.2 0.0 copy-done
  55.2 0.0 copy-start.1
  55.2 0.7 %copy.17 = bf16[1,128,1024]{2,1,0:T(8,128)(2,1)} copy(bf16[1,128,1024]{2,1,0:T(8,128)(2,1)S(1)} %bitcast.13) | data formatting | bytes 524288
  56.0 0.3 copy-done.1
  56.2 0.0 copy-start.2
  56.2 0.7 %copy.18 = bf16[1,1,64,1024]{3,2,1,0:T(8,128)(2,1)} copy(bf16[1,1,64,1024]{3,2,1,0:T(8,128)(2,1)S(1)} %bitcast.15) | data formatting | bytes 262144
  56.9 0.0 copy-done.2
  56.9 0.5 copy.19
Async XLA Ops:
  52.9 2.3 %copy-start = (bf16[128,1024]{1,0:T(8,128)(2,1)S(1)}, bf16[128,1024]{1,0:T(8,128)(2,1)}, u32[]{:S(2)}) copy-start(bf16[128,1024]{1,0:T(8,128)(2,1)} %get-tuple-element.9) | copy-start | bytes 786436
  55.2 1.0 %copy-start.1 = (bf16[64,1024]{1,0:T(8,128)(2,1)S(1)}, bf16[64,1024]{1,0:T(8,128)(2,1)}, u32[]{:S(2)}) copy-start(bf16[64,1024]{1,0:T(8,128)(2,1)} %get-tuple-element.10) | copy-start | bytes 393220
  56.2 0.7 %copy-start.2 = (f32[1,32]{1,0:T(1,128)S(1)}, f32[1,32]{1,0:T(1,128)}, u32[]{:S(2)}) copy-start(f32[1,32]{1,0:T(1,128)} %get-tuple-element.11) | copy-start | bytes 388

commit v2 on v1

--- a/solution.py
+++ b/solution.py
@@ -64,9 +64,9 @@
     c_hbm,
     m_hbm,
     g_hbm,
-    qg_hbm,
-    cg_hbm,
-    mg_hbm,
+    qg_buf,
+    cg_buf,
+    mg_buf,
     gt_ref,
     q_buf,
     g_buf,
@@ -83,13 +83,12 @@
     bias_ref,
     cbias_ref,
     has_ref,
+    xw_ref,
+    raw_ref,
     tanh_ref,
     gacc_ref,
     mt_ref,
     kt_ref,
-    qg_buf,
-    cg_buf,
-    mg_buf,
     to_cur,
     to_prev,
     red_cur,
@@ -191,8 +190,8 @@
     load_own.start()
     load_g.start()
 
-    offset = off_ref[0, 0]
-    flag_own[...] = jnp.where(jnp.full(flag_own.shape, offset, jnp.int32) < tok_rows, 1.0, 0.0)
+    offset = off_ref[...]
+    flag_own[...] = jnp.where(jnp.broadcast_to(offset, flag_own.shape) < tok_rows, 1.0, 0.0)
     pl.semaphore_wait(barrier, len(greeted))
 
     flags = [remote(flag_own, flag_buf.at[d - 1], in_block(block, d)) for d in range(1, BLOCK)]
@@ -280,13 +279,6 @@
     for copy in onward + gather:
         copy.start()
 
-    halo.wait_recv()
-
-    @pl.loop(0, groups)
-    def _(group):
-        self_forward(0, group)
-
-    is_owner = own_flag > 0.5
     has_prev = jnp.maximum(earlier, jnp.where(block > 0, 1.0, 0.0))
     local_row = row_id.astype(F32)
     image_col = col_id < image_rows
@@ -297,6 +289,12 @@
         cbias_ref[half] = (jnp.where(image_col, use_prev, use_own) - 1.0) * (-HIDDEN)
         has_ref[half] = jnp.maximum(use_own, use_prev)
 
+    halo.wait_recv()
+
+    @pl.loop(0, groups)
+    def _(group):
+        self_forward(0, group)
+
     for copy in gather + onward:
         copy.wait_recv()
     load_g.wait()
@@ -304,40 +302,25 @@
         earlier * cur_buf[...].astype(F32) + (1.0 - earlier) * prev_buf[...].astype(F32)
     ).astype(BF16)
 
-    def cross_half(half, group, key, value):
+    def cross_forward(half, group, key, value):
         self_out = so_ref[half, group]
         grad_out = stacked(g_buf, half, group, repeat)
-        scores = dot_nt(self_out, key).reshape(repeat, WINDOW, 2 * image_rows) + cbias_ref[half][None]
-        weights = softmax(scores.reshape(tall, 2 * image_rows)).reshape(
-            repeat, WINDOW, 2 * image_rows
-        )
-        narrow = weights.astype(BF16)
-        raw = dot_nt(grad_out, value).reshape(repeat, WINDOW, 2 * image_rows)
-        has = has_ref[half][None]
-        gate_sum = jnp.sum(narrow.astype(F32) * raw * has, axis=1)
-        factor = has * tanh_ref[pl.ds(pl.multiple_of(group * repeat, repeat), repeat), :][:, None, :]
-        grad_wide = grad_out.astype(F32)
-        grad_cross = (grad_wide.reshape(factor.shape) * factor).astype(BF16).reshape(tall, HEAD_DIM)
-        grad_weights = raw * factor
-        delta = jnp.sum(weights * grad_weights, axis=-1, keepdims=True)
-        grad_scores = (
-            (weights * (grad_weights - delta)).astype(BF16).reshape(tall, 2 * image_rows)
-        )
-        query_grad = dot_nn(grad_scores, key) * SCALE
-        gs_ref[half, group] = (grad_wide + query_grad).astype(BF16)
-        key_term = dot_tn(grad_scores, self_out)
-        value_term = dot_tn(narrow.reshape(tall, 2 * image_rows), grad_cross)
-        return gate_sum, key_term, value_term
+        scores = dot_nt(self_out, key).reshape(repeat, WINDOW, 2 * image_rows)
+        weights = softmax((scores + cbias_ref[half][None]).reshape(tall, 2 * image_rows))
+        raw = dot_nt(grad_out, value)
+        xw_ref[half, group] = weights
+        raw_ref[half, group] = raw
+        terms = (weights.astype(BF16).astype(F32) * raw).reshape(repeat, WINDOW, 2 * image_rows)
+        return jnp.sum(terms * has_ref[half][None], axis=1)
 
     @pl.loop(0, groups)
     def _(group):
         key = images[:, columns(group)]
         value = images[:, columns(group, key_width)]
-        first = cross_half(0, group, key, value)
-        second = cross_half(1, group, key, value)
-        gacc_ref[pl.ds(pl.multiple_of(group * repeat, repeat), repeat), :] = first[0] + second[0]
-        mt_ref[:, columns(group)] = (first[1] + second[1]) * SCALE
-        mt_ref[:, columns(group, key_width)] = first[2] + second[2]
+        own_heads = pl.ds(pl.multiple_of(group * repeat, repeat), repeat)
+        gacc_ref[own_heads, :] = cross_forward(0, group, key, value) + cross_forward(
+            1, group, key, value
+        )
 
     totals = jnp.sum(gacc_ref[...], axis=1, keepdims=True)
     spread = lax.broadcasted_iota(jnp.int32, (heads, 128), 0) == lax.broadcasted_iota(
@@ -348,6 +331,28 @@
     ga = [remote(ga_own, ga_in.at[d - 1], row_peer(d)) for d in range(1, ROW)]
     for copy in ga:
         copy.start()
+
+    def cross_backward(half, group, key):
+        self_out = so_ref[half, group]
+        grad_out = stacked(g_buf, half, group, repeat).astype(F32)
+        weights = xw_ref[half, group]
+        own_heads = pl.ds(pl.multiple_of(group * repeat, repeat), repeat)
+        factor = has_ref[half][None] * tanh_ref[own_heads, :][:, None, :]
+        factor = factor.reshape(tall, 2 * image_rows)
+        grad_cross = (grad_out * factor).astype(BF16)
+        grad_weights = raw_ref[half, group] * factor
+        delta = jnp.sum(weights * grad_weights, axis=-1, keepdims=True)
+        grad_scores = (weights * (grad_weights - delta)).astype(BF16)
+        gs_ref[half, group] = (grad_out + dot_nn(grad_scores, key) * SCALE).astype(BF16)
+        return dot_tn(grad_scores, self_out), dot_tn(weights.astype(BF16), grad_cross)
+
+    @pl.loop(0, groups)
+    def _(group):
+        key = images[:, columns(group)]
+        first = cross_backward(0, group, key)
+        second = cross_backward(1, group, key)
+        mt_ref[:, columns(group)] = (first[0] + second[0]) * SCALE
+        mt_ref[:, columns(group, key_width)] = first[1] + second[1]
 
     carried = mt_ref[0:image_rows, :]
     to_cur[...] = (carried * earlier).astype(BF16)
@@ -363,6 +368,16 @@
         remote(to_cur.at[part(d)], red_cur.at[d - 1], in_block(block, d)) for d in range(1, BLOCK)
     ]
     for copy in reduce_prev + reduce_cur:
+        copy.start()
+
+    for copy in ga:
+        copy.wait_recv()
+    gate_line = ga_own[...]
+    for d in range(1, ROW):
+        gate_line = gate_line + ga_in[d - 1]
+    gb_own[...] = gate_line
+    gb = [remote(gb_own, gb_in.at[d - 1], y_peer(d)) for d in range(1, y_count)]
+    for copy in gb:
         copy.start()
 
     def self_backward(half, group):
@@ -388,23 +403,20 @@
     @pl.loop(0, groups)
     def _(group):
         self_backward(0, group)
+        self_backward(1, group)
 
     halo_out[...] = kt_ref[0, 0:WINDOW, :].astype(BF16)
     halo_back = remote(halo_out, halo_in, on_seq(lax.rem(me + shards - 1, shards)))
     halo_back.start()
-    out_low = pltpu.make_async_copy(
-        qg_buf.at[pl.ds(0, WINDOW)], qg_hbm.at[pl.ds(0, WINDOW)], local_sem.at[4]
-    )
-    out_low.start()
-
-    for copy in ga:
-        copy.wait_recv()
-    gate_line = ga_own[...]
-    for d in range(1, ROW):
-        gate_line = gate_line + ga_in[d - 1]
-    gb_own[...] = gate_line
-    gb = [remote(gb_own, gb_in.at[d - 1], y_peer(d)) for d in range(1, y_count)]
+
     for copy in gb:
+        copy.wait_recv()
+    gate_line = gb_own[...]
+    for d in range(1, y_count):
+        gate_line = gate_line + gb_in[d - 1]
+    gc_own[...] = gate_line
+    gc = [remote(gc_own, gc_in.at[d - 1], z_peer(d)) for d in range(1, z_count)]
+    for copy in gc:
         copy.start()
 
     for copy in reduce_cur + reduce_prev:
@@ -419,40 +431,17 @@
     for copy in give:
         copy.start()
 
-    @pl.loop(0, groups)
-    def _(group):
-        self_backward(1, group)
-
-    out_high = pltpu.make_async_copy(
-        qg_buf.at[pl.ds(WINDOW, WINDOW)], qg_hbm.at[pl.ds(WINDOW, WINDOW)], local_sem.at[5]
-    )
-    out_high.start()
-
-    for copy in gb:
-        copy.wait_recv()
-    gate_line = gb_own[...]
-    for d in range(1, y_count):
-        gate_line = gate_line + gb_in[d - 1]
-    gc_own[...] = gate_line
-    gc = [remote(gc_own, gc_in.at[d - 1], z_peer(d)) for d in range(1, z_count)]
-    for copy in gc:
-        copy.start()
-
     halo_back.wait_recv()
     cg_buf[0:WINDOW, :] = (kt_ref[0, WINDOW : 2 * WINDOW, :] + kt_ref[1, 0:WINDOW, :]).astype(BF16)
     cg_buf[WINDOW : 2 * WINDOW, :] = (
         kt_ref[1, WINDOW : 2 * WINDOW, :] + halo_in[...].astype(F32)
     ).astype(BF16)
-    out_context = pltpu.make_async_copy(cg_buf, cg_hbm, local_sem.at[6])
-    out_context.start()
 
     for copy in give:
         copy.wait_recv()
     mg_buf[...] = (
         (mt_ref[image_rows : 2 * image_rows, :] + sum_buf[...].astype(F32)) * own_flag
     ).astype(BF16)
-    out_memory = pltpu.make_async_copy(mg_buf, mg_hbm, local_sem.at[7])
-    out_memory.start()
 
     for copy in gc:
         copy.wait_recv()
@@ -467,10 +456,6 @@
         + [halo_back] + gb + give + gc
     ):
         copy.wait_send()
-    out_low.wait()
-    out_high.wait()
-    out_context.wait()
-    out_memory.wait()
 
 
 def on_device(shards, docs, queries, context, segment_start, memory, image_offset, cross_gate, out_grad):
@@ -487,7 +472,6 @@
     copies = 3 + 3 + 1 + 3 + 4 + (ROW - 1) + 4 + 3 + 1 + (y_count - 1) + 3 + (z_count - 1)
     anywhere = pl.BlockSpec(memory_space=pl.ANY)
     vmem = pl.BlockSpec(memory_space=pltpu.VMEM)
-    smem = pl.BlockSpec(memory_space=pltpu.SMEM)
 
     def buf(*shape):
         return pltpu.VMEM(shape, BF16)
@@ -498,13 +482,13 @@
     query_grad, context_grad, memory_grad, gate_grad = pl.pallas_call(
         functools.partial(kernel, shards, docs),
         out_shape=(
-            jax.ShapeDtypeStruct((tok_rows, model), BF16),
-            jax.ShapeDtypeStruct((tok_rows, width), BF16),
-            jax.ShapeDtypeStruct((image_rows, width), BF16),
-            jax.ShapeDtypeStruct((1, heads), F32),
+            pltpu.VMEM((tok_rows, model), BF16),
+            pltpu.VMEM((tok_rows, width), BF16),
+            pltpu.VMEM((image_rows, width), BF16),
+            pltpu.VMEM((1, heads), F32),
         ),
-        in_specs=[vmem, smem, vmem, anywhere, anywhere, anywhere, anywhere],
-        out_specs=(anywhere, anywhere, anywhere, vmem),
+        in_specs=[vmem, vmem, vmem, anywhere, anywhere, anywhere, anywhere],
+        out_specs=(vmem, vmem, vmem, vmem),
         scratch_shapes=[
             buf(tok_rows, model),
             buf(tok_rows, model),
@@ -521,13 +505,12 @@
             wide(2, WINDOW, 2 * WINDOW),
             wide(2, WINDOW, 2 * image_rows),
             wide(2, WINDOW, 2 * image_rows),
+            wide(2, groups, tall, 2 * image_rows),
+            wide(2, groups, tall, 2 * image_rows),
             wide(heads, 128),
             wide(heads, 128),
             wide(2 * image_rows, width),
             wide(2, 2 * WINDOW, width),
-            buf(tok_rows, model),
-            buf(tok_rows, width),
-            buf(image_rows, width),
             buf(image_rows, width),
             buf(image_rows, width),
             buf(BLOCK - 1, quarter, width),
@@ -541,7 +524,7 @@
             wide(max(y_count - 1, 1), 8, 128),
             wide(8, 128),
             wide(max(z_count - 1, 1), 8, 128),
-            pltpu.SemaphoreType.DMA((8,)),
+            pltpu.SemaphoreType.DMA((4,)),
             pltpu.SemaphoreType.DMA((copies,)),
             pltpu.SemaphoreType.DMA((copies,)),
         ],

time: 57.6 us -> 53.3 us (0.925)
  Pallas kernels: 51.6 us -> 49 us
  local copies, waits for them, and re-layouts: 4.51 us -> 2.84 us
    pallas_call x1, Pallas kernels: 51.6 us -> 49 us  [on_device(): pl.pallas_call(functools.partial(kernel, shards, docs), out_shape=(pltpu....]
    unnamed x10 -> x4, local copies, waits for them, and re-layouts: 4.51 us -> 2.84 us
where the time goes in v2:
time: 53.3 us; the launch traced here: 53.1 us
  Pallas kernels  49 us (92%)
  local copies, waits for them, and re-layouts  2.84 us (5%)
  between operations  1.29 us (2%)
    pallas_call x1, Pallas kernels, on_device(): pl.pallas_call(functools.partial(kernel, shards, docs), out_shape=(pltpu....  49 us
    unnamed x4, local copies, waits for them, and re-layouts  2.84 us

profile of v2, /device:TPU:1, one launch (start us, length us, event | category | flops | bytes accessed | tf_op | source)
XLA Modules:
  0.0 53.1 jit_solution(13747186855689022153)
XLA Ops:
  1.3 49.0 %shard_map.102 = (bf16[128,4096]{1,0:T(8,128)(2,1)S(1)}, bf16[128,1024]{1,0:T(8,128)(2,1)S(1)}, bf16[64,1024]{1,0:T(8,128)(2,1)S(1)}, f32[1,32]{1,0:T(1,128)S(1)}) custom-call(s32[1,128]{1,0:T(1,128)} %seg_ref.1, s32[1,1]{1,0:T(1,128)S(6)} %copy.19.off_ref, f32[1,32]{1,0:T(1,128)} %bitcast.17, bf16[128,4096]{1,0:T(8,128)(2,1)} %bitcast.13, ...), custom_call_target="tpu_custom_call" | custom-call | tf_op jit(solution)/shard_map/pallas_call | solution.py:482
  50.3 1.0 %copy.15 = bf16[1,128,4096]{2,1,0:T(8,128)(2,1)} copy(bf16[1,128,4096]{2,1,0:T(8,128)(2,1)S(1)} %bitcast.9) | data formatting | bytes 2097152
  51.2 0.7 %copy.16 = bf16[1,128,1024]{2,1,0:T(8,128)(2,1)} copy(bf16[1,128,1024]{2,1,0:T(8,128)(2,1)S(1)} %bitcast.10) | data formatting | bytes 524288
  51.9 0.5 copy.18
  52.5 0.7 %copy.17 = bf16[1,1,64,1024]{3,2,1,0:T(8,128)(2,1)} copy(bf16[1,1,64,1024]{3,2,1,0:T(8,128)(2,1)S(1)} %bitcast.11) | data formatting | bytes 262144
